TPU v7x, 256 devices: a whole 4x4x8 slice. The times are simulated.
256 devices in a mesh: seq: 16 (over y, z_hi), fsdp: 16 (over x, z_lo, core).
Axes of the slice: x: 4, y: 4, z: 8 (z_hi: 4, z_lo: 2; z = z_hi * 2 + z_lo), core: 2. Of those that a mesh axis runs over, the one named last changes fastest.
Arguments:
- tokens: bfloat16 [2048, 4096], P('seq', 'fsdp'), may hold values from -6 to 6
- in_weight: bfloat16 [3, 4096, 4096], P(None, 'seq', 'fsdp'), may hold values from -0.09375 to 0.09375
- out_weight: bfloat16 [4096, 4096], P('fsdp', 'seq'), may hold values from -0.09375 to 0.09375
- filters: float32 [4096, 128], P('fsdp'), may hold values from -0.5 to 0.5
- cotangent: bfloat16 [2048, 4096], P('seq', 'fsdp'), may hold values from -6 to 6
Outputs:
- mixed_out: bfloat16 [2048, 4096], P('seq', 'fsdp')
- grad_tokens: bfloat16 [2048, 4096], P('seq', 'fsdp')
- grad_in_weight: float32 [3, 4096, 4096], P(None, 'seq', 'fsdp')
- grad_out_weight: float32 [4096, 4096], P('fsdp', 'seq')
- grad_filters: float32 [4096, 128], P('fsdp')
All inputs are finite; a program needn't handle non-finite values.
Results may differ from a plain program's by a relative error of at most 0.018.
Values may be sent and summed in bfloat16 or wider, within the bound.
A program may use at most 64 MiB of HBM per device.

v0:
```python
import jax
import jax.numpy as jnp
from jax import lax
from jax.sharding import PartitionSpec as P

highest = lax.Precision.HIGHEST


def from_behind(value, axis, by):
    length = lax.axis_size(axis)
    pairs = [(i, i + by) for i in range(length) if 0 <= i + by < length]
    return lax.ppermute(value, axis, pairs)


def causal_filter(extended, filters):
    kernel = jnp.flip(jnp.transpose(filters), 0)[:, None, :]
    result = lax.conv_general_dilated(
        extended[None],
        kernel,
        (1,),
        "VALID",
        dimension_numbers=("NWC", "WIO", "NWC"),
        feature_group_count=filters.shape[0],
        precision=highest,
    )
    return result[0]


def reverse_filter(extended, filters):
    kernel = jnp.transpose(filters)[:, None, :]
    result = lax.conv_general_dilated(
        extended[None],
        kernel,
        (1,),
        "VALID",
        dimension_numbers=("NWC", "WIO", "NWC"),
        feature_group_count=filters.shape[0],
        precision=highest,
    )
    return result[0]


def filter_grad(extended, gradient):
    result = lax.conv_general_dilated(
        extended[None],
        gradient[:, None, :],
        (1,),
        "VALID",
        dimension_numbers=("NWC", "WIO", "NWC"),
        feature_group_count=gradient.shape[1],
        precision=highest,
    )
    return jnp.transpose(jnp.flip(result[0], 0))


def on_device(tokens, in_weight, out_weight, filters, cotangent):
    margin = filters.shape[1] - 1
    gathered = lax.all_gather(tokens, "fsdp", axis=1, tiled=True)
    out_full = lax.all_gather(out_weight, "seq", axis=1, tiled=True)
    in_full = lax.all_gather(in_weight, "seq", axis=1, tiled=True)
    projected = jnp.einsum("td,idc->itc", gathered, in_full, preferred_element_type=jnp.float32)
    projected = projected.astype(jnp.bfloat16)
    queries = projected[0].astype(jnp.float32)
    key_part = projected[1].astype(jnp.float32)
    value_part = projected[2].astype(jnp.float32)
    signal = (key_part * value_part).astype(jnp.bfloat16)
    earlier = from_behind(signal[-margin:], "seq", 1)
    extended = jnp.concatenate([earlier, signal], 0).astype(jnp.float32)
    filtered = causal_filter(extended, filters)
    gated_rows = (queries * filtered).astype(jnp.bfloat16)
    partial_value = jnp.dot(gated_rows, out_full, preferred_element_type=jnp.float32)
    mixed_out = lax.psum_scatter(
        partial_value.astype(jnp.bfloat16), "fsdp", scatter_dimension=1, tiled=True
    )
    grad_full = lax.all_gather(cotangent, "fsdp", axis=1, tiled=True)
    grad_gated = lax.dot_general(
        grad_full, out_full, (((1,), (1,)), ((), ())), preferred_element_type=jnp.float32
    )
    grad_queries = grad_gated * filtered
    grad_filtered = (grad_gated * queries).astype(jnp.bfloat16)
    later_rows = from_behind(grad_filtered[:margin], "seq", -1)
    grad_signal = reverse_filter(
        jnp.concatenate([grad_filtered, later_rows], 0).astype(jnp.float32), filters
    )
    grad_filters = lax.psum(
        filter_grad(extended, grad_filtered.astype(jnp.float32)).astype(jnp.bfloat16), "seq"
    ).astype(jnp.float32)
    grad_projected = jnp.stack(
        [grad_queries, grad_signal * value_part, grad_signal * key_part]
    ).astype(jnp.bfloat16)
    grad_partial = jnp.einsum(
        "itc,idc->td", grad_projected, in_full, preferred_element_type=jnp.float32
    )
    grad_tokens = lax.psum_scatter(
        grad_partial.astype(jnp.bfloat16), "fsdp", scatter_dimension=1, tiled=True
    )
    weight_in_part = jnp.einsum(
        "td,itc->idc", gathered, grad_projected, preferred_element_type=jnp.float32
    )
    weight_out_part = lax.dot_general(
        gated_rows, grad_full, (((0,), (0,)), ((), ())), preferred_element_type=jnp.float32
    )
    grad_in_weight, grad_out_weight = (
        lax.psum_scatter(
            weight_in_part.astype(jnp.bfloat16), "seq", scatter_dimension=1, tiled=True
        ).astype(jnp.float32),
        lax.psum_scatter(
            weight_out_part.astype(jnp.bfloat16), "seq", scatter_dimension=1, tiled=True
        ).astype(jnp.float32),
    )
    return (mixed_out, grad_tokens, grad_in_weight, grad_out_weight, grad_filters)


def solution(mesh):
    placed = (
        P("seq", "fsdp"),
        P(None, "seq", "fsdp"),
        P("fsdp", "seq"),
        P("fsdp", None),
        P("seq", "fsdp"),
    )
    return jax.shard_map(
        on_device,
        mesh=mesh,
        in_specs=placed,
        out_specs=(
            P("seq", "fsdp"),
            P("seq", "fsdp"),
            P(None, "seq", "fsdp"),
            P("fsdp", "seq"),
            P("fsdp", None),
        ),
        check_vma=False,
    )
```

profile of v0, /device:TPU:64, one launch (start us, length us, event | category | flops | bytes accessed | tf_op | source)
XLA Modules:
  0.0 766.3 jit_solution(3096591360201777987)
XLA Ops:
  7.2 0.0 all-gather.7.cloned.1.call-start
  7.2 0.7 all-gather.7.cloned.1.call-update
  7.9 0.0 all-gather.5.cloned.1.call-start
  7.9 0.7 all-gather.5.cloned.1.call-update
  8.6 0.0 all-gather.11.cloned.1.call-start
  8.7 0.7 all-gather.11.cloned.1.call-update
  9.4 0.0 all-gather.9.cloned.1.call-start
  9.4 0.5 all-gather.9.cloned.1.call-update
  10.0 0.0 copy-start.3
  10.0 0.0 all-reduce.2.cloned.1.call-start
  10.0 38.2 %all-gather.7.cloned.1.call-done = bf16[128,4096]{1,0:T(8,128)(2,1)} async-done(((bf16[128,256]{1,0:T(8,128)(2,1)}), bf16[128,4096]{1,0:T(8,128)(2,1)}) %all-gather.7.cloned.1.call-update) | async-done | bytes 1048592 | tf_op jit(solution)/shard_map/all_gather | solution.py:58
  48.2 99.6 %all-gather.5.cloned.1.call-done = bf16[3,4096,256]{2,1,0:T(8,128)(2,1)} async-done(((bf16[3,256,256]{2,1,0:T(8,128)(2,1)}), bf16[3,4096,256]{2,1,0:T(8,128)(2,1)}) %all-gather.5.cloned.1.call-update) | async-done | bytes 6291472 | tf_op jit(solution)/shard_map/all_gather | solution.py:60
  147.8 4.1 fusion.2
  151.9 32.4 %all-gather.11.cloned.1.call-done = bf16[128,4096]{1,0:T(8,128)(2,1)} async-done(((bf16[128,256]{1,0:T(8,128)(2,1)}), bf16[128,4096]{1,0:T(8,128)(2,1)}) %all-gather.11.cloned.1.call-update) | async-done | bytes 1048592 | tf_op jit(solution)/shard_map/all_gather | solution.py:75
  184.3 64.7 %all-gather.9.cloned.1.call-done = bf16[256,4096]{1,0:T(8,128)(2,1)} async-done(((bf16[256,256]{1,0:T(8,128)(2,1)}), bf16[256,4096]{1,0:T(8,128)(2,1)}) %all-gather.9.cloned.1.call-update) | async-done | bytes 2097168 | tf_op jit(solution)/shard_map/all_gather | solution.py:59
  249.0 2.8 fusion.15
  251.7 2.1 collective-permute-start.1
  253.8 0.0 copy-done.3
  253.8 0.1 copy.13
  254.0 6.5 collective-permute-done.1
  260.5 1.4 fusion.5
  262.0 1.9 collective-permute-start
  263.9 0.2 rev.7
  264.1 0.1 copy.11
  264.2 4.8 collective-permute-done
  269.1 1.4 fusion.9
  270.5 0.0 copy-start.2
  270.5 1.9 fusion.7
  272.3 0.0 copy-start.1
  272.4 0.7 rev.8
  273.1 0.0 all-reduce.2.cloned.1.call-update
  273.1 0.0 reduce-scatter.11.cloned.1.call-start
  273.1 0.0 copy-done.2
  273.1 2.0 convolution_convert_fusion.1
  275.2 0.0 reduce-scatter.11.cloned.1.call-update
  275.2 0.0 reduce-scatter.9.cloned.1.call-start
  275.3 0.0 copy-done.1
  275.3 4.4 fusion
  279.7 0.0 reduce-scatter.9.cloned.1.call-update
  279.8 0.0 copy-start
  279.8 0.0 reduce-scatter.7.cloned.1.call-start
  279.8 6.0 fusion.1
  285.9 0.0 reduce-scatter.7.cloned.1.call-update
  285.9 0.0 reduce-scatter.5.cloned.1.call-start
  285.9 0.0 copy-done
  285.9 1.5 convolution_convert_fusion.2
  287.4 0.0 reduce-scatter.5.cloned.1.call-update
  287.4 137.7 %all-reduce.2.cloned.1.call-done = bf16[256,128]{0,1:T(8,128)(2,1)} async-done(((bf16[256,128]{0,1:T(8,128)(2,1)}), bf16[256,128]{0,1:T(8,128)(2,1)}) %all-reduce.2.cloned.1.call-update) | async-done | bytes 65552 | tf_op jit(solution)/shard_map/psum | solution.py:85
  425.1 1.6 copy.20
  426.7 87.7 %reduce-scatter.11.cloned.1.call-done = bf16[256,256]{1,0:T(8,128)(2,1)} async-done(((bf16[256,4096]{1,0:T(8,128)(2,1)}), bf16[256,256]{1,0:T(8,128)(2,1)}) %reduce-scatter.11.cloned.1.call-update) | async-done | bytes 131088 | tf_op jit(solution)/shard_map/reduce_scatter | solution.py:107
  514.4 1.6 convert_element_type.84
  516.0 110.7 %reduce-scatter.9.cloned.1.call-done = bf16[3,256,256]{1,2,0:T(8,128)(2,1)} async-done(((bf16[3,4096,256]{1,2,0:T(8,128)(2,1)}), bf16[3,256,256]{1,2,0:T(8,128)(2,1)}) %reduce-scatter.9.cloned.1.call-update) | async-done | bytes 393232 | tf_op jit(solution)/shard_map/reduce_scatter | solution.py:104
  626.7 2.0 copy.19
  628.8 65.0 %reduce-scatter.7.cloned.1.call-done = bf16[128,256]{1,0:T(8,128)(2,1)} async-done(((bf16[128,4096]{1,0:T(8,128)(2,1)}), bf16[128,256]{1,0:T(8,128)(2,1)}) %reduce-scatter.7.cloned.1.call-update) | async-done | bytes 65552 | tf_op jit(solution)/shard_map/reduce_scatter | solution.py:94
  693.8 66.0 %reduce-scatter.5.cloned.1.call-done = bf16[128,256]{1,0:T(8,128)(2,1)} async-done(((bf16[128,4096]{1,0:T(8,128)(2,1)}), bf16[128,256]{1,0:T(8,128)(2,1)}) %reduce-scatter.5.cloned.1.call-update) | async-done | bytes 65552 | tf_op jit(solution)/shard_map/reduce_scatter | solution.py:72
  (6 shorter events, 0.1 us)
Async XLA Ops:
  7.2 41.0 %all-gather.7.cloned.1.call-start = ((), (), s32[]{:S(2)}) async-start(), calls=%async_computation.5 | async-start | bytes 1114112 | tf_op jit(solution)/shard_map/all_gather | solution.py:58
  7.9 139.9 %all-gather.5.cloned.1.call-start = ((), (), s32[]{:S(2)}) async-start(), calls=%async_computation.4 | async-start | bytes 6684672 | tf_op jit(solution)/shard_map/all_gather | solution.py:60
  8.6 175.6 %all-gather.11.cloned.1.call-start = ((), (), s32[]{:S(2)}) async-start(), calls=%async_computation.8 | async-start | bytes 1114112 | tf_op jit(solution)/shard_map/all_gather | solution.py:75
  9.4 239.6 %all-gather.9.cloned.1.call-start = ((), (), s32[]{:S(2)}) async-start(), calls=%async_computation.6 | async-start | bytes 2228224 | tf_op jit(solution)/shard_map/all_gather | solution.py:59
  10.0 243.9 %copy-start.3 = (f32[256,128]{1,0:T(8,128)S(1)}, f32[256,128]{1,0:T(8,128)}, u32[]{:S(2)}) copy-start(f32[256,128]{1,0:T(8,128)} %param.8) | copy-start | bytes 393220
  10.0 415.1 %all-reduce.2.cloned.1.call-start = ((), (), s32[]{:S(2)}) async-start(), calls=%async_computation.12 | async-start | bytes 131072 | tf_op jit(solution)/shard_map/psum | solution.py:85
  251.7 8.7 %collective-permute-start.1 = (bf16[127,256]{1,0:T(8,128)(2,1)S(1)}, bf16[127,256]{1,0:T(8,128)(2,1)S(1)}, u32[]{:S(2)}, u32[]{:S(2)}) collective-permute-start(bf16[127,256]{1,0:T(8,128)(2,1)S(1)} %bitcast.66), channel_id=1, source_target_pairs={{16,0},{32,16},{48,32},{64,48},{80,64},{96,80},{112,96},{128,112},... | collective-permute-start | bytes 195080 | tf_op jit(solution)/shard_map/ppermute | solution.py:12
  262.0 7.1 collective-permute-start
  270.5 2.7 copy-start.2
  272.3 2.9 copy-start.1
  273.1 241.3 %reduce-scatter.11.cloned.1.call-start = ((), (), s32[]{:S(2)}) async-start(), calls=%async_computation.11 | async-start | bytes 2228224 | tf_op jit(solution)/shard_map/reduce_scatter | solution.py:107
  275.2 351.5 %reduce-scatter.9.cloned.1.call-start = ((), (), s32[]{:S(2)}) async-start(), calls=%async_computation.10 | async-start | bytes 6684672 | tf_op jit(solution)/shard_map/reduce_scatter | solution.py:104
  279.8 6.2 copy-start
  279.8 414.0 %reduce-scatter.7.cloned.1.call-start = ((), (), s32[]{:S(2)}) async-start(), calls=%async_computation.9 | async-start | bytes 1114112 | tf_op jit(solution)/shard_map/reduce_scatter | solution.py:94
  285.9 473.9 %reduce-scatter.5.cloned.1.call-start = ((), (), s32[]{:S(2)}) async-start(), calls=%async_computation.7 | async-start | bytes 1114112 | tf_op jit(solution)/shard_map/reduce_scatter | solution.py:72
Sparse Core Ops, SparseCore 0:
  9.7 38.4 all-gather.6
  50.7 97.0 all-gather.4
  149.6 34.6 all-gather.10
  186.5 62.4 all-gather.8
  273.2 151.8 all-reduce.1
  428.5 85.7 reduce-scatter.10
  518.1 108.5 reduce-scatter.8
  629.8 63.9 reduce-scatter.6
  696.9 62.8 reduce-scatter.4
where the time goes:
time: 767 us; the launch traced here: 766 us
  waiting for transfers between devices  716 us (93%)
  matrix products  25.5 us (3%)
  between operations  14 us (2%)
    psum x1, waiting for transfers between devices, on_device(): lax.psum(filter_grad(extended, grad_filtered.astype(jnp.float32)).astype(...  138 us
    reduce_scatter x1, waiting for transfers between devices, on_device(): lax.psum_scatter(weight_in_part.astype(jnp.bfloat16), 'seq', scatter_dime...  111 us
    all_gather x1, waiting for transfers between devices, on_device(): in_full = lax.all_gather(in_weight, 'seq', axis=1, tiled=True)  99.6 us
    reduce_scatter x1, waiting for transfers between devices, on_device(): lax.psum_scatter(weight_out_part.astype(jnp.bfloat16), 'seq', scatter_dim...  87.7 us
    reduce_scatter x1, waiting for transfers between devices, on_device(): lax.psum_scatter(partial_value.astype(jnp.bfloat16), 'fsdp', scatter_dime...  66 us
    reduce_scatter x1, waiting for transfers between devices, on_device(): lax.psum_scatter(grad_partial.astype(jnp.bfloat16), 'fsdp', scatter_dimen...  65 us
    all_gather x1, waiting for transfers between devices, on_device(): out_full = lax.all_gather(out_weight, 'seq', axis=1, tiled=True)  64.7 us
    all_gather x1, waiting for transfers between devices, on_device(): gathered = lax.all_gather(tokens, 'fsdp', axis=1, tiled=True)  38.2 us
  transfers between devices with their start and end apart: 11, of which 11 were waited for; matrix products, arithmetic and copies ran while one was open for 3% of the time, Pallas kernels for 0%

commit v1 on v0

v1 whole, which is shorter than its diff:
```python
import functools

import jax
import jax.numpy as jnp
from jax import lax
from jax.experimental import pallas as pl
from jax.experimental.pallas import tpu as pltpu

highest = lax.Precision.HIGHEST
MESH = pl.DeviceIdType.MESH
f32 = jnp.float32
bf16 = jnp.bfloat16


class Place:
    def __init__(self):
        self.s = lax.axis_index("seq")
        self.f = lax.axis_index("fsdp")
        self.y, self.zh = self.s // 4, self.s % 4
        self.x, self.w = self.f // 4, self.f % 4
        self.zl, self.core = self.w // 2, self.w % 2

    def y_at(self, step):
        return (self.y + 4 + step) % 4

    def z_at(self, step):
        return (self.zh + 4 + step) % 4

    def x_at(self, step):
        return (self.x + 4 + step) % 4

    def y_dev(self, step):
        return (self.y_at(step) * 4 + self.zh, self.f)

    def z_dev(self, step):
        return (self.y * 4 + self.z_at(step), self.f)

    def x_dev(self, step):
        return (self.s, self.x_at(step) * 4 + self.w)

    def other_core(self):
        return (self.s, self.f + 1 - 2 * self.core)

    def s_dev(self, step):
        return ((self.s + 16 + step) % 16, self.f)

    def spread(self, zl):
        return (self.y * 4 + self.w, self.x * 4 + zl * 2 + self.zh % 2)

    def origin(self, half):
        return (self.y * 4 + half * 2 + self.core, self.x * 4 + self.zh)

    def is_me(self, dev):
        return jnp.logical_and(dev[0] == self.s, dev[1] == self.f)


def pos(a):
    return (a % 2) * 2 + a // 2


class Net:
    def __init__(self, place, send, recv):
        self.place, self.send, self.recv = place, send, recv
        self.n_send = self.n_recv = 0
        self.ends = []

    def slots(self, count):
        first = self.n_recv
        self.n_recv += count
        return first

    def copy(self, src, dst, dev, slot=None, may_be_me=False):
        if slot is None:
            slot = self.slots(1)
        out = self.send.at[self.n_send]
        self.n_send += 1
        far = pltpu.make_async_remote_copy(
            src_ref=src, dst_ref=dst, send_sem=out, recv_sem=self.recv.at[slot],
            device_id=dev, device_id_type=MESH,
        )
        if may_be_me:
            me = self.place.is_me(dev)
            near = pltpu.make_async_copy(src, dst, self.recv.at[slot])
            pl.when(me)(near.start)
            pl.when(jnp.logical_not(me))(far.start)
            self.ends.append(lambda: pl.when(jnp.logical_not(me))(far.wait_send))
        else:
            far.start()
            self.ends.append(far.wait_send)
        return far

    def arrived(self, ref, slot):
        pltpu.make_async_copy(ref, ref, self.recv.at[slot]).wait()

    def finish(self):
        for end in self.ends:
            end()


def meet(others):
    barrier = pltpu.get_barrier_semaphore()
    for dev in others:
        pl.semaphore_signal(barrier, inc=1, device_id=dev, device_id_type=MESH)
    pl.semaphore_wait(barrier, len(others))


class RingGather:
    def __init__(self, net, dev, at, block, half, own):
        self.net, self.dev, self.at, self.block, self.half = net, dev, at, block, half
        here = block(at(0))
        self.up = net.copy(own, here, dev(1))
        self.down = net.copy(own, here, dev(-1))

    def relay(self):
        self.up.wait_recv()
        self.far_up = self.net.copy(
            self.half(self.at(-1), 0), self.half(self.at(-1), 0), self.dev(1))
        self.down.wait_recv()
        self.far_down = self.net.copy(
            self.half(self.at(1), 1), self.half(self.at(1), 1), self.dev(-1))

    def wait(self):
        self.far_up.wait_recv()
        self.far_down.wait_recv()


class RingReduce:
    def __init__(self, net, dev, at, out, far_in, near_in, cut):
        self.net, self.dev, self.at = net, dev, at
        self.out, self.far_in, self.near_in, self.cut = out, far_in, near_in, cut

    def start_far(self, value):
        self.out[0] = value.astype(bf16)
        a, b = self.cut
        self.f_up = self.net.copy(self.out.at[(0,) + a], self.far_in.at[0], self.dev(1))
        self.f_down = self.net.copy(self.out.at[(0,) + b], self.far_in.at[1], self.dev(-1))

    def start_near(self, up, down):
        self.read_up, self.read_down = up, down
        a, b = self.cut
        self.out[(1,) + b] = up(b).astype(bf16)
        self.n_up = self.net.copy(self.out.at[(1,) + b], self.near_in.at[(0,) + b], self.dev(1))
        self.out[(2,) + a] = down(a).astype(bf16)
        self.n_down = self.net.copy(self.out.at[(2,) + a], self.near_in.at[(1,) + a], self.dev(-1))

    def relay(self):
        a, b = self.cut
        self.f_up.wait_recv()
        self.out[(1,) + a] = (self.read_up(a) + self.far_in[0].astype(f32)).astype(bf16)
        self.r_up = self.net.copy(self.out.at[(1,) + a], self.near_in.at[(0,) + a], self.dev(1))
        self.f_down.wait_recv()
        self.out[(2,) + b] = (self.read_down(b) + self.far_in[1].astype(f32)).astype(bf16)
        self.r_down = self.net.copy(self.out.at[(2,) + b], self.near_in.at[(1,) + b], self.dev(-1))

    def result(self, own):
        for copy in (self.n_up, self.n_down, self.r_up, self.r_down):
            copy.wait_recv()
        return own + self.near_in[0].astype(f32) + self.near_in[1].astype(f32)


class Activations:
    def __init__(self, net, place, own, full):
        self.net, self.place, self.full = net, place, full
        self.first = net.slots(2)
        self.core_copies = []
        for zl in range(2):
            net.copy(own, full.at[place.x, pos(place.zh)], place.spread(zl),
                     slot=self.first + place.zh // 2, may_be_me=True)

    def unit(self, b, lo=0, n=2):
        return self.full.at[b, pl.ds(self.place.core * 2 + lo, n)]

    def to_core(self, ref):
        self.core_copies.append(self.net.copy(ref, ref, self.place.other_core()))

    def ring(self):
        place = self.place
        for half in range(2):
            self.net.arrived(self.full.at[place.x, place.core * 2 + half], self.first + half)
        self.gather = RingGather(
            self.net, place.x_dev, place.x_at, self.unit,
            lambda b, h: self.unit(b, h, 1), self.unit(place.x))
        self.to_core(self.unit(place.x))

    def relay(self):
        self.gather.relay()
        self.to_core(self.unit(self.place.x_at(-1)))
        self.to_core(self.unit(self.place.x_at(1)))

    def far(self):
        self.gather.wait()
        self.to_core(self.unit(self.place.x_at(2)))

    def wait(self):
        for copy in self.core_copies:
            copy.wait_recv()


def dot(a, b, ca, cb):
    return lax.dot_general(a, b, (((ca,), (cb,)), ((), ())), preferred_element_type=f32)


def rows512(value):
    return value.reshape(512, 256)


def forward_kernel(tok, cot, win, wout,
                   kvq_o, gg_o, sig_o, gf_o, xg_o, cg_o, wg_o, wo_o,
                   xg, cg, wg, wo, part, z_out, z_far, z_near, halo, mine, send, recv, local):
    place = Place()
    near = [place.y_dev(1), place.y_dev(-1), place.z_dev(1), place.z_dev(-1), place.x_dev(1),
            place.x_dev(-1), place.other_core(), place.s_dev(1), place.s_dev(-1)]
    far = [place.spread(0), place.spread(1), place.origin(0), place.origin(1)]
    meet(near + far)
    net = Net(place, send, recv)

    xs = Activations(net, place, tok, xg)
    half_rows = (pl.ds(0, 128), pl.ds(128, 128))

    def weight(own, full):
        return RingGather(net, place.y_dev, place.y_at, lambda b: full.at[b],
                          lambda b, h: full.at[b, half_rows[h]], own)

    wk = weight(win.at[1], wg.at[1])
    cs = Activations(net, place, cot, cg)
    wv = weight(win.at[2], wg.at[2])
    wu = weight(wout, wo)
    wq = weight(win.at[0], wg.at[0])
    for i in range(3):
        wg[i, place.y] = win[i]
    wo[place.y] = wout[...]

    xs.ring()
    cs.ring()
    wk.relay()
    xs.relay()
    wv.relay()
    cs.relay()
    wu.relay()
    wq.relay()
    xs.far()
    cs.far()

    cut = ((pl.ds(0, 64),), (pl.ds(64, 64),))

    def reduce(slot, left, right, transposed):
        total = None
        for b in range(4):
            term = dot(rows512(left[b]), right(b), 1, 1 if transposed else 0)
            total = term if total is None else total + term
        part[slot] = total.reshape(4, 128, 256)
        ring = RingReduce(net, place.z_dev, place.z_at, z_out.at[slot], z_far.at[slot],
                          z_near.at[slot], cut)
        ring.start_far(part[slot, pos(place.z_at(2))])
        ring.start_near(lambda rows: part[(slot, pos(place.z_at(1))) + rows],
                        lambda rows: part[(slot, pos(place.z_at(-1))) + rows])
        return ring

    stores = []

    def keep(src, dst):
        copy = pltpu.make_async_copy(src, dst, local.at[len(stores)])
        copy.start()
        stores.append(copy)

    xs.wait()
    keep(xg, xg_o)
    wk.wait()
    rk = reduce(0, xg, lambda b: wg[1, b], False)
    wv.wait()
    rv = reduce(1, xg, lambda b: wg[2, b], False)
    rk.relay()
    cs.wait()
    keep(cg, cg_o)
    wu.wait()
    keep(wo, wo_o)
    ru = reduce(2, cg, lambda b: wo[b], True)
    rv.relay()
    wq.wait()
    keep(wg, wg_o)
    rq = reduce(3, xg, lambda b: wg[0, b], False)
    me = pos(place.zh)
    k = rk.result(part[0, me]).astype(bf16)
    ru.relay()
    v = rv.result(part[1, me]).astype(bf16)
    kvq_o[0] = k
    kvq_o[1] = v
    mine[0] = (k.astype(f32) * v.astype(f32)).astype(bf16)
    after = net.copy(mine.at[0], halo.at[0], place.s_dev(1))
    rq.relay()
    gg = ru.result(part[2, me])
    gg_o[...] = gg
    q = rq.result(part[3, me]).astype(bf16)
    kvq_o[2] = q
    mine[1] = (gg * q.astype(f32)).astype(bf16)
    before = net.copy(mine.at[1], halo.at[1], place.s_dev(-1))
    sig_o[1] = mine[0]
    gf_o[0] = mine[1]
    after.wait_recv()
    sig_o[0] = jnp.where(place.s == 0, jnp.zeros((128, 256), bf16), halo[0])
    before.wait_recv()
    gf_o[1] = jnp.where(place.s == 15, jnp.zeros((128, 256), bf16), halo[1])
    for copy in stores:
        copy.wait()
    net.finish()


def backward_kernel(gated, gp, gfilt, xg_i, cg_i, wg_i, wo_i,
                    mixed_o, gtok_o, gin_o, gout_o, gfilt_o,
                    xg, cg, wg, wo, ag, keep_g, y_out, y_far, y_near,
                    part, c_out, c_in, x_out, x_far, x_near, fin_out, fin_in,
                    fz_out, fz_far, fz_near, fy, fz, send, recv, local):
    place = Place()
    near = [place.y_dev(1), place.y_dev(-1), place.z_dev(1), place.z_dev(-1), place.x_dev(1),
            place.x_dev(-1), place.other_core()]
    far = [place.spread(0), place.spread(1), place.origin(0), place.origin(1)]
    loads = []
    for src, dst in ((wo_i, wo), (cg_i, cg), (xg_i, xg), (wg_i, wg)):
        copy = pltpu.make_async_copy(src, dst, local.at[len(loads)])
        copy.start()
        loads.append(copy)
    meet(near + far)
    net = Net(place, send, recv)

    half_rows = (pl.ds(0, 64), pl.ds(64, 64))

    def acts(own, i):
        full = ag.at[i]
        return RingGather(net, place.z_dev, place.z_at, lambda a: full.at[pos(a)],
                          lambda a, h: full.at[pos(a), half_rows[h]], own)

    gathers = [acts(gated, 0)] + [acts(gp.at[i], i + 1) for i in range(3)]
    ag[0, pos(place.zh)] = gated[...]
    for i in range(3):
        ag[i + 1, pos(place.zh)] = gp[i]

    y_cut = ((pl.ds(0, 128),), (pl.ds(128, 128),))

    def weight_grad(slot, block):
        ring = RingReduce(net, place.y_dev, place.y_at, y_out.at[slot], y_far.at[slot],
                          y_near.at[slot], y_cut)
        ring.start_far(block(place.y_at(2)))
        keep_g[slot, 0] = block(place.y_at(1))
        keep_g[slot, 1] = block(place.y_at(-1))
        ring.start_near(lambda rows: keep_g[(slot, 0) + rows], lambda rows: keep_g[(slot, 1) + rows])
        keep_g[slot, 2] = block(place.y_at(0))
        return ring

    x_cut = ((pl.ds(0, 1),), (pl.ds(1, 1),))

    class Features:
        def __init__(self, slot, block):
            self.slot, self.swaps = slot, []
            for j, step in enumerate((2, 1, -1, 0)):
                part[slot, j] = block(place.x_at(step)).reshape(4, 128, 256)
                c_out[slot, j] = part[slot, j, pl.ds((1 - place.core) * 2, 2)].astype(bf16)
                self.swaps.append(net.copy(c_out.at[slot, j], c_in.at[slot, j], place.other_core()))

        def both(self, j, rows=None):
            base = place.core * 2
            if rows is None:
                return part[self.slot, j, pl.ds(base, 2)] + c_in[self.slot, j].astype(f32)
            lo = rows[0].start
            return (part[self.slot, j, pl.ds(base + lo, 1)]
                    + c_in[self.slot, j, pl.ds(lo, 1)].astype(f32))

        def ring(self):
            slot = self.slot
            self.reduce = RingReduce(net, place.x_dev, place.x_at, x_out.at[slot], x_far.at[slot],
                                     x_near.at[slot], x_cut)
            self.swaps[0].wait_recv()
            self.reduce.start_far(self.both(0))
            self.swaps[1].wait_recv()
            self.swaps[2].wait_recv()
            self.reduce.start_near(lambda rows: self.both(1, rows), lambda rows: self.both(2, rows))

        def relay(self):
            self.reduce.relay()

        def last(self):
            slot = self.slot
            self.swaps[3].wait_recv()
            fin_out[slot] = self.reduce.result(self.both(3)).astype(bf16)
            self.first = net.slots(2)
            for half in range(2):
                net.copy(fin_out.at[slot, half], fin_in.at[slot, place.zl], place.origin(half),
                         slot=self.first + place.zl, may_be_me=True)

        def result(self):
            for zl in range(2):
                net.arrived(fin_in.at[self.slot, zl], self.first + zl)
            return (fin_in[self.slot, 0].astype(f32) + fin_in[self.slot, 1].astype(f32)).astype(bf16)

    f_cut = ((pl.ds(0, 32),), (pl.ds(32, 32),))
    fr = RingReduce(net, place.z_dev, place.z_at, fz_out, fz_far, fz_near, f_cut)
    fr.start_far(gfilt[place.z_at(2)])
    fr.start_near(lambda rows: gfilt[(place.z_at(1),) + rows],
                  lambda rows: gfilt[(place.z_at(-1),) + rows])

    gathers[0].relay()
    gathers[1].relay()
    gathers[0].wait()
    loads[0].wait()
    loads[1].wait()
    mixed = Features(0, lambda b: dot(rows512(ag[0]), wo[b], 1, 0))
    grads = [weight_grad(0, lambda b: dot(rows512(ag[0]), rows512(cg[b]), 0, 0))]
    gathers[2].relay()
    fr.relay()
    gathers[1].wait()
    loads[2].wait()

    def in_grad(i):
        return weight_grad(i + 1, lambda b: dot(rows512(xg[b]), rows512(ag[i + 1]), 0, 0))

    grads.append(in_grad(0))
    mixed.ring()
    gathers[3].relay()
    gathers[2].wait()
    grads.append(in_grad(1))
    grads[0].relay()
    mixed.relay()
    fy[place.y] = fr.result(gfilt[place.zh]).astype(bf16)
    fyg = RingGather(net, place.y_dev, place.y_at, lambda b: fy.at[b],
                     lambda b, h: fy.at[b, (pl.ds(0, 32), pl.ds(32, 32))[h]], fy.at[place.y])
    gathers[3].wait()
    loads[3].wait()

    def token_block(b):
        total = dot(rows512(ag[1]), wg[0, b], 1, 1)
        for i in (1, 2):
            total = total + dot(rows512(ag[i + 1]), wg[i, b], 1, 1)
        return total

    gtok = Features(1, token_block)
    grads.append(in_grad(2))
    grads[1].relay()
    mixed.last()
    gtok.ring()
    fyg.relay()
    grads[2].relay()
    gtok.relay()
    grads[3].relay()
    gout_o[...] = grads[0].result(keep_g[0, 2])
    gin_o[0] = grads[1].result(keep_g[1, 2])
    fyg.wait()
    fz[place.zh] = (fy[0].astype(f32) + fy[1].astype(f32) + fy[2].astype(f32)
                    + fy[3].astype(f32)).astype(bf16)
    fzg = RingGather(net, place.z_dev, place.z_at, lambda b: fz.at[b],
                     lambda b, h: fz.at[b, (pl.ds(0, 32), pl.ds(32, 32))[h]], fz.at[place.zh])
    gtok.last()
    fzg.relay()
    mixed_o[...] = mixed.result()
    gin_o[1] = grads[2].result(keep_g[2, 2])
    gin_o[2] = grads[3].result(keep_g[3, 2])
    fzg.wait()
    gfilt_o[...] = fz[...].astype(f32)
    gtok_o[...] = gtok.result()
    net.finish()


def vmem(*shape, kind=bf16):
    return pltpu.VMEM(shape, kind)


def shape_of(*shape, kind=bf16):
    return jax.ShapeDtypeStruct(shape, kind)


def in_vmem():
    return pl.BlockSpec(memory_space=pltpu.VMEM)


def in_place():
    return pl.BlockSpec(memory_space=pl.ANY)


def forward(tokens, cotangent, in_weight, out_weight):
    return pl.pallas_call(
        forward_kernel,
        out_shape=(
            shape_of(3, 128, 256), shape_of(128, 256, kind=f32), shape_of(2, 128, 256),
            shape_of(2, 128, 256), shape_of(4, 4, 128, 256), shape_of(4, 4, 128, 256),
            shape_of(3, 4, 256, 256), shape_of(4, 256, 256)),
        in_specs=[in_vmem()] * 4,
        out_specs=(in_vmem(),) * 4 + (in_place(),) * 4,
        scratch_shapes=[
            vmem(4, 4, 128, 256), vmem(4, 4, 128, 256), vmem(3, 4, 256, 256), vmem(4, 256, 256),
            vmem(4, 4, 128, 256, kind=f32), vmem(4, 3, 128, 256), vmem(4, 2, 64, 256),
            vmem(4, 2, 128, 256), vmem(2, 128, 256), vmem(2, 128, 256),
            pltpu.SemaphoreType.DMA((80,)), pltpu.SemaphoreType.DMA((80,)),
            pltpu.SemaphoreType.DMA((4,))],
        compiler_params=pltpu.CompilerParams(
            collective_id=0, has_side_effects=True, vmem_limit_bytes=56 * 2 ** 20),
        name="forward_exchange",
    )(tokens, cotangent, in_weight, out_weight)


def backward(gated, gp, gfilt, xg, cg, wg, wo):
    return pl.pallas_call(
        backward_kernel,
        out_shape=(
            shape_of(128, 256), shape_of(128, 256), shape_of(3, 256, 256, kind=f32),
            shape_of(256, 256, kind=f32), shape_of(4, 64, 128, kind=f32)),
        in_specs=[in_vmem()] * 3 + [in_place()] * 4,
        out_specs=(in_vmem(),) * 5,
        scratch_shapes=[
            vmem(4, 4, 128, 256), vmem(4, 4, 128, 256), vmem(3, 4, 256, 256), vmem(4, 256, 256),
            vmem(4, 4, 128, 256), vmem(4, 3, 256, 256, kind=f32), vmem(4, 3, 256, 256),
            vmem(4, 2, 128, 256), vmem(4, 2, 256, 256),
            vmem(2, 4, 4, 128, 256, kind=f32), vmem(2, 4, 2, 128, 256), vmem(2, 4, 2, 128, 256),
            vmem(2, 3, 2, 128, 256), vmem(2, 2, 1, 128, 256), vmem(2, 2, 2, 128, 256),
            vmem(2, 2, 128, 256), vmem(2, 2, 128, 256),
            vmem(3, 64, 128), vmem(2, 32, 128), vmem(2, 64, 128), vmem(4, 64, 128),
            vmem(4, 64, 128),
            pltpu.SemaphoreType.DMA((96,)), pltpu.SemaphoreType.DMA((96,)),
            pltpu.SemaphoreType.DMA((4,))],
        compiler_params=pltpu.CompilerParams(
            collective_id=1, has_side_effects=True, vmem_limit_bytes=56 * 2 ** 20),
        name="backward_exchange",
    )(gated, gp, gfilt, xg, cg, wg, wo)


def causal_filter(extended, filters):
    kernel = jnp.flip(jnp.transpose(filters), 0)[:, None, :]
    result = lax.conv_general_dilated(
        extended[None], kernel, (1,), "VALID", dimension_numbers=("NWC", "WIO", "NWC"),
        feature_group_count=filters.shape[0], precision=highest)
    return result[0]


def reverse_filter(extended, filters):
    kernel = jnp.transpose(filters)[:, None, :]
    result = lax.conv_general_dilated(
        extended[None], kernel, (1,), "VALID", dimension_numbers=("NWC", "WIO", "NWC"),
        feature_group_count=filters.shape[0], precision=highest)
    return result[0]


def filter_grad(extended, gradient):
    result = lax.conv_general_dilated(
        extended[None], gradient[:, None, :], (1,), "VALID",
        dimension_numbers=("NWC", "WIO", "NWC"), feature_group_count=gradient.shape[1],
        precision=highest)
    return jnp.transpose(jnp.flip(result[0], 0))


def on_device(tokens, in_weight, out_weight, filters, cotangent):
    kvq, grad_gated, signal, grads, xg, cg, wg, wo = forward(
        tokens, cotangent, in_weight, out_weight)
    key_part, value_part, queries = (kvq[i].astype(f32) for i in range(3))
    extended = signal.reshape(256, 256).astype(f32)[1:]
    later = grads.reshape(256, 256).astype(f32)[:-1]
    filtered = causal_filter(extended, filters)
    gated = (queries * filtered).astype(bf16)
    grad_signal = reverse_filter(later, filters)
    grad_filters = filter_grad(extended, grads[0].astype(f32))
    grad_projected = jnp.stack(
        [grad_gated * filtered, grad_signal * value_part, grad_signal * key_part]).astype(bf16)
    mixed, grad_tokens, grad_in, grad_out, grad_filters = backward(
        gated, grad_projected, grad_filters.reshape(4, 64, 128), xg, cg, wg, wo)
    return mixed, grad_tokens, grad_in, grad_out, grad_filters.reshape(256, 128)


def solution(mesh):
    placed = (
        jax.P("seq", "fsdp"),
        jax.P(None, "seq", "fsdp"),
        jax.P("fsdp", "seq"),
        jax.P("fsdp", None),
        jax.P("seq", "fsdp"),
    )
    return jax.shard_map(
        on_device,
        mesh=mesh,
        in_specs=placed,
        out_specs=(
            jax.P("seq", "fsdp"),
            jax.P("seq", "fsdp"),
            jax.P(None, "seq", "fsdp"),
            jax.P("fsdp", "seq"),
            jax.P("fsdp", None),
        ),
        check_vma=False,
    )
```

time: 767 us -> 125 us (0.16)
  waiting for transfers between devices: 716 us -> 0 us
  Pallas kernels: 0 us -> 107 us
  matrix products: 25.5 us -> 4.67 us
  between operations: 14 us -> 0.77 us
    reduce_scatter x4 -> x0, waiting for transfers between devices: 329 us -> none  [the longest x1 111 us: on_device(): lax.psum_scatter(weight_in_part.astype(jnp.bfloat16), 'seq', scatter_dime...]
    all_gather x4 -> x0, waiting for transfers between devices: 235 us -> none  [the longest x1 99.6 us: on_device(): in_full = lax.all_gather(in_weight, 'seq', axis=1, tiled=True)]
    psum x1 -> x0, waiting for transfers between devices: 138 us -> none  [on_device(): lax.psum(filter_grad(extended, grad_filtered.astype(jnp.float32)).astype(...]
    pallas_call x0 -> x2, Pallas kernels: none -> 107 us  [the longest x1 54.6 us: forward(): pl.pallas_call(forward_kernel, out_shape=(shape_of(3, 128, 256), shape_of...]
    dot_general x6 -> x0, matrix products: 20.8 us -> none  [the longest x1 6.03 us: on_device(): jnp.einsum('itc,idc->td', grad_projected, in_full, preferred_element_type...]
    ppermute x2 -> x0, waiting for transfers between devices: 11.3 us -> none  [from_behind(): return lax.ppermute(value, axis, pairs)]
  transfers between devices with their start and end apart: 11 -> 0, of which waited for: 11 -> 0; matrix products, arithmetic and copies ran while one was open for 3% -> 0% of each run, Pallas kernels for 0% -> 0%
where the time goes in v1:
time: 125 us; the launch traced here: 124 us
  Pallas kernels  107 us (86%)
  local copies, waits for them, and re-layouts  10.4 us (8%)
  matrix products  4.67 us (4%)
  other arithmetic  1.39 us (1%)
    pallas_call x1, Pallas kernels, forward(): pl.pallas_call(forward_kernel, out_shape=(shape_of(3, 128, 256), shape_of...  54.6 us
    pallas_call x1, Pallas kernels, backward(): pl.pallas_call(backward_kernel, out_shape=(shape_of(128, 256), shape_of(1...  52.4 us
    unnamed x16, local copies, waits for them, and re-layouts  6.44 us

profile of v1, /device:TPU:64, one launch (start us, length us, event | category | flops | bytes accessed | tf_op | source)
XLA Modules:
  0.0 124.2 jit_solution(7042582748465001287)
XLA Ops:
  0.6 1.0 rev.7
  1.6 0.1 copy.17
  1.8 1.0 copy.19
  2.8 54.6 %forward_exchange.1 = (bf16[3,128,256]{2,1,0:T(8,128)(2,1)}, f32[128,256]{1,0:T(8,128)}, bf16[2,128,256]{2,1,0:T(8,128)(2,1)}, bf16[2,128,256]{2,1,0:T(8,128)(2,...) custom-call(bf16[128,256]{1,0:T(8,128)(2,1)} %tok.1, ...), custom_call_target="tpu_custom_call" | custom-call | tf_op jit(solution)/shard_map/forward_exchange/pallas_call | solution.py:478
  57.4 0.9 slice_bitcast_fusion.1
  58.4 0.0 copy-start.2
  58.4 0.0 copy-start.3
  58.4 0.0 copy-start
  58.4 1.4 %fusion.4 = f32[1,128,256]{2,0,1:T(1,128)S(1)} fusion(f32[128,1,256]{2,1,0:T(1,128)S(1)} %copy.17, bf16[1,255,256]{2,1,0:T(8,128)(2,1)S(1)} %slice_bitcast_fusion.1), kind=kOutput, calls=%fused_computation.4 | convolution fusion | flops 50331648 | bytes 392704 | tf_op jit(solution)/shard_map/conv_general_dilated | solution.py:525
  59.8 0.0 copy-done.2
  59.8 0.0 copy-done.3
  59.8 0.7 fusion.9
  60.5 0.0 copy-done
  60.5 1.9 %fusion.2 = f32[1,128,256]{2,0,1:T(1,128)S(1)} fusion(bf16[1,255,256]{2,1,0:T(8,128)(2,1)S(1)} %slice_bitcast_fusion.1, bf16[128,1,256]{2,0,1:T(8,128)(2,1)S(1)} %slice_bitcast_fusion.2), kind=kOutput, calls=%fused_computation.2 | convolution fusion | flops 8388608 | bytes 327168 | tf_op jit(solution)/shard_map/conv_general_dilated | solution.py:540
  62.4 0.1 rev.8
  62.5 0.8 copy.24
  63.2 1.4 %fusion = f32[1,128,256]{2,0,1:T(1,128)S(1)} fusion(f32[128,1,256]{2,1,0:T(1,128)S(1)} %copy.19, bf16[1,255,256]{2,1,0:T(8,128)(2,1)S(1)} %slice_bitcast_fusion), kind=kOutput, calls=%fused_computation | convolution fusion | flops 50331648 | bytes 392704 | tf_op jit(solution)/shard_map/conv_general_dilated | solution.py:533
  64.7 0.7 pad_maximum_fusion.gp
  65.4 52.4 %backward_exchange.1 = (bf16[128,256]{1,0:T(8,128)(2,1)}, bf16[128,256]{1,0:T(8,128)(2,1)}, f32[3,256,256]{2,1,0:T(8,128)}, f32[256,256]{1,0:T(8,128)}, f32[4,64,128]{2,1,0:T(8,128)}) custom-call(bf16[128,256]{1,0:T(8,128)(2,1)} %get-tuple-element.34.gated, bf16[3,128,256]{2,1,0:T(8,128)(2,1)} %pad_maximum_fusion.gp, f32[4,64,128]{2,1,0:T(8,128)} %bitcast.34, ...), custom_call_target="tpu_custom_call" | custom-call | tf_op jit(solution)/shard_map/backward_exchange/pallas_call | solution.py:499
  117.8 0.0 copy-start.1
  117.8 0.0 copy-start.4
  117.8 1.5 %copy.48 = bf16[128,256]{1,0:T(8,128)(2,1)} copy(bf16[128,256]{1,0:T(8,128)(2,1)} %get-tuple-element.40) | data formatting | bytes 131072
  119.3 1.5 %copy.49 = bf16[128,256]{1,0:T(8,128)(2,1)} copy(bf16[128,256]{1,0:T(8,128)(2,1)} %get-tuple-element.41) | data formatting | bytes 131072
  120.8 2.1 %copy.50 = f32[3,256,256]{2,1,0:T(8,128)} copy(f32[3,256,256]{2,1,0:T(8,128)} %get-tuple-element.42) | data formatting | bytes 1572864
  122.8 0.0 copy-done.1
  122.8 0.7 copy.51
  123.5 0.0 copy-done.4
  123.5 0.7 copy.52
  (4 shorter events, 0.1 us)
Async XLA Ops:
  58.4 1.4 %copy-start.2 = (bf16[3,128,256]{2,1,0:T(8,128)(2,1)S(1)}, bf16[3,128,256]{2,1,0:T(8,128)(2,1)}, u32[]{:S(2)}) copy-start(bf16[3,128,256]{2,1,0:T(8,128)(2,1)} %get-tuple-element.18) | copy-start | bytes 589828
  58.4 1.4 %copy-start.3 = (f32[128,256]{1,0:T(8,128)S(1)}, f32[128,256]{1,0:T(8,128)}, u32[]{:S(2)}) copy-start(f32[128,256]{1,0:T(8,128)} %get-tuple-element.20) | copy-start | bytes 393220
  58.4 2.1 %copy-start = (bf16[2,128,256]{2,1,0:T(8,128)(2,1)S(1)}, bf16[2,128,256]{2,1,0:T(8,128)(2,1)}, u32[]{:S(2)}) copy-start(bf16[2,128,256]{2,1,0:T(8,128)(2,1)} %get-tuple-element.21) | copy-start | bytes 393220
  117.8 5.1 %copy-start.1 = (f32[256,256]{1,0:T(8,128)S(1)}, f32[256,256]{1,0:T(8,128)}, u32[]{:S(2)}) copy-start(f32[256,256]{1,0:T(8,128)} %get-tuple-element.43) | copy-start | bytes 786436
  117.8 5.8 %copy-start.4 = (f32[4,64,128]{2,1,0:T(8,128)S(1)}, f32[4,64,128]{2,1,0:T(8,128)}, u32[]{:S(2)}) copy-start(f32[4,64,128]{2,1,0:T(8,128)} %get-tuple-element.30) | copy-start | bytes 393220

commit v2 on v1

v2 whole, which is shorter than its diff:
```python
import functools

import jax
import jax.numpy as jnp
from jax import lax
from jax.experimental import pallas as pl
from jax.experimental.pallas import tpu as pltpu

MESH = pl.DeviceIdType.MESH
f32 = jnp.float32
bf16 = jnp.bfloat16


class Place:
    def __init__(self):
        self.s = lax.axis_index("seq")
        self.f = lax.axis_index("fsdp")
        self.y, self.zh = self.s // 4, self.s % 4
        self.x, self.w = self.f // 4, self.f % 4
        self.zl, self.core = self.w // 2, self.w % 2

    def y_at(self, step):
        return (self.y + 4 + step) % 4

    def z_at(self, step):
        return (self.zh + 4 + step) % 4

    def x_at(self, step):
        return (self.x + 4 + step) % 4

    def y_dev(self, step):
        return (self.y_at(step) * 4 + self.zh, self.f)

    def z_dev(self, step):
        return (self.y * 4 + self.z_at(step), self.f)

    def x_dev(self, step):
        return (self.s, self.x_at(step) * 4 + self.w)

    def other_core(self):
        return (self.s, self.f + 1 - 2 * self.core)

    def s_dev(self, step):
        return ((self.s + 16 + step) % 16, self.f)

    def spread(self, zl):
        return (self.y * 4 + self.w, self.x * 4 + zl * 2 + self.zh % 2)

    def origin(self, half):
        return (self.y * 4 + half * 2 + self.core, self.x * 4 + self.zh)

    def is_me(self, dev):
        return jnp.logical_and(dev[0] == self.s, dev[1] == self.f)


def pos(a):
    return (a % 2) * 2 + a // 2


class Net:
    def __init__(self, place, send, recv):
        self.place, self.send, self.recv = place, send, recv
        self.n_send = self.n_recv = 0
        self.ends = []

    def slots(self, count):
        first = self.n_recv
        self.n_recv += count
        return first

    def copy(self, src, dst, dev, slot=None, may_be_me=False):
        if slot is None:
            slot = self.slots(1)
        out = self.send.at[self.n_send]
        self.n_send += 1
        far = pltpu.make_async_remote_copy(
            src_ref=src, dst_ref=dst, send_sem=out, recv_sem=self.recv.at[slot],
            device_id=dev, device_id_type=MESH,
        )
        if may_be_me:
            me = self.place.is_me(dev)
            near = pltpu.make_async_copy(src, dst, self.recv.at[slot])
            pl.when(me)(near.start)
            pl.when(jnp.logical_not(me))(far.start)
            self.ends.append(lambda: pl.when(jnp.logical_not(me))(far.wait_send))
        else:
            far.start()
            self.ends.append(far.wait_send)
        return far

    def arrived(self, ref, slot):
        pltpu.make_async_copy(ref, ref, self.recv.at[slot]).wait()

    def finish(self):
        for end in self.ends:
            end()


def meet(others):
    barrier = pltpu.get_barrier_semaphore()
    for dev in others:
        pl.semaphore_signal(barrier, inc=1, device_id=dev, device_id_type=MESH)
    pl.semaphore_wait(barrier, len(others))


class RingGather:
    def __init__(self, net, dev, at, block, half, own):
        self.net, self.dev, self.at, self.block, self.half = net, dev, at, block, half
        here = block(at(0))
        self.up = net.copy(own, here, dev(1))
        self.down = net.copy(own, here, dev(-1))

    def relay(self):
        self.up.wait_recv()
        self.far_up = self.net.copy(
            self.half(self.at(-1), 0), self.half(self.at(-1), 0), self.dev(1))
        self.down.wait_recv()
        self.far_down = self.net.copy(
            self.half(self.at(1), 1), self.half(self.at(1), 1), self.dev(-1))

    def wait(self):
        self.far_up.wait_recv()
        self.far_down.wait_recv()


class RingReduce:
    def __init__(self, net, dev, at, out, far_in, near_in, cut):
        self.net, self.dev, self.at = net, dev, at
        self.out, self.far_in, self.near_in, self.cut = out, far_in, near_in, cut

    def start_far(self, value):
        self.out[0] = value.astype(bf16)
        a, b = self.cut
        self.f_up = self.net.copy(self.out.at[(0,) + a], self.far_in.at[0], self.dev(1))
        self.f_down = self.net.copy(self.out.at[(0,) + b], self.far_in.at[1], self.dev(-1))

    def start_near(self, up, down):
        self.read_up, self.read_down = up, down
        a, b = self.cut
        self.out[(1,) + b] = up(b).astype(bf16)
        self.n_up = self.net.copy(self.out.at[(1,) + b], self.near_in.at[(0,) + b], self.dev(1))
        self.out[(2,) + a] = down(a).astype(bf16)
        self.n_down = self.net.copy(self.out.at[(2,) + a], self.near_in.at[(1,) + a], self.dev(-1))

    def relay(self):
        a, b = self.cut
        self.f_up.wait_recv()
        self.out[(1,) + a] = (self.read_up(a) + self.far_in[0].astype(f32)).astype(bf16)
        self.r_up = self.net.copy(self.out.at[(1,) + a], self.near_in.at[(0,) + a], self.dev(1))
        self.f_down.wait_recv()
        self.out[(2,) + b] = (self.read_down(b) + self.far_in[1].astype(f32)).astype(bf16)
        self.r_down = self.net.copy(self.out.at[(2,) + b], self.near_in.at[(1,) + b], self.dev(-1))

    def result(self, own):
        for copy in (self.n_up, self.n_down, self.r_up, self.r_down):
            copy.wait_recv()
        return own + self.near_in[0].astype(f32) + self.near_in[1].astype(f32)


class Activations:
    def __init__(self, net, place, own, full):
        self.net, self.place, self.full = net, place, full
        self.first = net.slots(2)
        self.core_copies = []
        for zl in range(2):
            net.copy(own, full.at[place.x, pos(place.zh)], place.spread(zl),
                     slot=self.first + place.zh // 2, may_be_me=True)

    def unit(self, b, lo=0, n=2):
        return self.full.at[b, pl.ds(self.place.core * 2 + lo, n)]

    def to_core(self, ref):
        self.core_copies.append(self.net.copy(ref, ref, self.place.other_core()))

    def ring(self):
        place = self.place
        for half in range(2):
            self.net.arrived(self.full.at[place.x, place.core * 2 + half], self.first + half)
        self.gather = RingGather(
            self.net, place.x_dev, place.x_at, self.unit,
            lambda b, h: self.unit(b, h, 1), self.unit(place.x))
        self.to_core(self.unit(place.x))

    def relay(self):
        self.gather.relay()
        self.to_core(self.unit(self.place.x_at(-1)))
        self.to_core(self.unit(self.place.x_at(1)))

    def far(self):
        self.gather.wait()
        self.to_core(self.unit(self.place.x_at(2)))

    def wait(self):
        for copy in self.core_copies:
            copy.wait_recv()


def dot(a, b, ca=1, cb=0):
    return lax.dot_general(a, b, (((ca,), (cb,)), ((), ())), preferred_element_type=f32)


def rows512(value):
    return value.reshape(512, 256)


def side_by_side(values):
    return jnp.concatenate(values, axis=1)


def filter_sum(taps, shifted, start):
    halves = []
    for h in range(2):
        def step(jj, total):
            eight = taps[h, jj]
            first = pl.multiple_of(start(jj), 8)
            for r in range(8):
                total = total + eight[r:r + 1] * shifted[r, h, pl.ds(first, 128)]
            return total
        halves.append(lax.fori_loop(0, 16, step, jnp.zeros((128, 128), f32)))
    return side_by_side(halves)


def block_kernel(tok, cot, win, wout, filters,
                 mixed_o, gtok_o, gin_o, gout_o, gfilt_o,
                 xg, cg, wg, wo, xt, part, z_out, z_far, z_near, halo, mine, kvq,
                 taps, ext, shifted, tap_grads, gfilt,
                 ag, keep_g, y_out, y_far, y_near, feat, c_out, c_in, x_out, x_far, x_near,
                 fin_out, fin_in, fz_out, fz_far, fz_near, fy, fz,
                 mixed_v, gtok_v, grads_v, gfilt_v, send, recv, local):
    place = Place()
    others = [place.y_dev(1), place.y_dev(-1), place.z_dev(1), place.z_dev(-1), place.x_dev(1),
              place.x_dev(-1), place.other_core(), place.s_dev(1), place.s_dev(-1),
              place.spread(0), place.spread(1), place.origin(0), place.origin(1)]
    meet(others)
    net = Net(place, send, recv)
    half_rows = (pl.ds(0, 128), pl.ds(128, 128))

    def weight(own, full):
        return RingGather(net, place.y_dev, place.y_at, lambda b: full.at[b],
                          lambda b, h: full.at[b, half_rows[h]], own)

    xs = Activations(net, place, tok, xg)
    wk = weight(win.at[1], wg.at[1])
    cs = Activations(net, place, cot, cg)
    wv = weight(win.at[2], wg.at[2])
    for i in range(3):
        wg[i, place.y] = win[i]
    wo[place.y] = wout[...]
    turned = jnp.transpose(filters[...])
    for h in range(2):
        taps[h] = turned[:, h * 128:(h + 1) * 128].reshape(16, 8, 128)

    cut = ((pl.ds(0, 64),), (pl.ds(64, 64),))

    def reduce(slot, left, right, transposed):
        total = dot(side_by_side([rows512(left[b]) for b in range(4)]), right,
                    1, 1 if transposed else 0)
        part[slot] = total.reshape(4, 128, 256)
        ring = RingReduce(net, place.z_dev, place.z_at, z_out.at[slot], z_far.at[slot],
                          z_near.at[slot], cut)
        ring.start_far(part[slot, pos(place.z_at(2))])
        ring.start_near(lambda rows: part[(slot, pos(place.z_at(1))) + rows],
                        lambda rows: part[(slot, pos(place.z_at(-1))) + rows])
        return ring

    def turn(b):
        xt[b] = jnp.transpose(rows512(xg[b]))

    xs.ring()
    wk.relay()
    wq = weight(win.at[0], wg.at[0])
    cs.ring()
    xs.relay()
    wv.relay()
    wu = weight(wout, wo)
    xs.far()
    wk.wait()
    xs.wait()
    rk = reduce(0, xg, wg[1].reshape(1024, 256), False)
    wq.relay()
    wv.wait()
    rv = reduce(1, xg, wg[2].reshape(1024, 256), False)
    cs.relay()
    rk.relay()
    wu.relay()
    cs.far()
    wq.wait()
    rq = reduce(2, xg, wg[0].reshape(1024, 256), False)
    rv.relay()
    cs.wait()
    wu.wait()
    ru = reduce(3, cg, side_by_side([wo[b] for b in range(4)]), True)
    me = pos(place.zh)
    k = rk.result(part[0, me]).astype(bf16)
    kvq[0] = k
    rq.relay()
    v = rv.result(part[1, me]).astype(bf16)
    kvq[1] = v
    signal = (k.astype(f32) * v.astype(f32)).astype(bf16)
    mine[0] = signal
    after = net.copy(mine.at[0], halo.at[0], place.s_dev(1))

    def extend(lo, value):
        value = value.astype(f32)
        for h in range(2):
            ext[h, lo:lo + 128] = value[:, h * 128:(h + 1) * 128]

    extend(128, signal)
    turn(0)
    ru.relay()
    turn(1)
    after.wait_recv()
    extend(0, jnp.where(place.s == 0, jnp.zeros((128, 256), bf16), halo[0]))
    for r in range(8):
        for h in range(2):
            shifted[r, h, 8:256] = ext[h, 8 - r:256 - r]
    filtered = filter_sum(taps, shifted, lambda jj: 128 - 8 * jj)
    q = rq.result(part[2, me]).astype(bf16)

    quarter = (pl.ds(0, 64), pl.ds(64, 64))

    def acts(i, value):
        full = ag.at[i]
        full[me] = value.astype(bf16)
        return RingGather(net, place.z_dev, place.z_at, lambda a: full.at[pos(a)],
                          lambda a, h: full.at[pos(a), quarter[h]], full.at[me])

    gathers = [acts(0, q.astype(f32) * filtered)]
    gg = ru.result(part[3, me])
    grad_filtered = (gg * q.astype(f32)).astype(bf16)
    mine[1] = grad_filtered
    before = net.copy(mine.at[1], halo.at[1], place.s_dev(-1))
    gathers.append(acts(1, gg * filtered))

    gradient = grad_filtered.astype(f32)
    for h in range(2):
        side = gradient[:, h * 128:(h + 1) * 128]

        def one(jj, unused):
            first = pl.multiple_of(128 - 8 * jj, 8)
            tap_grads[h, jj] = jnp.concatenate(
                [jnp.sum(side * shifted[r, h, pl.ds(first, 128)], axis=0, keepdims=True)
                 for r in range(8)], axis=0)
            return unused
        lax.fori_loop(0, 16, one, 0)
    gathers[0].relay()
    extend(0, mine[1])
    before.wait_recv()
    extend(128, jnp.where(place.s == 15, jnp.zeros((128, 256), bf16), halo[1]))
    for r in range(8):
        for h in range(2):
            shifted[r, h, 0:248] = ext[h, r:248 + r]
    grad_signal = filter_sum(taps, shifted, lambda jj: 8 * jj)
    gathers.append(acts(2, grad_signal * kvq[1].astype(f32)))
    gathers[1].relay()
    gathers.append(acts(3, grad_signal * kvq[0].astype(f32)))

    f_cut = ((pl.ds(0, 32),), (pl.ds(32, 32),))
    for h in range(2):
        turned = jnp.transpose(tap_grads[h].reshape(128, 128))
        gfilt[2 * h] = turned[0:64]
        gfilt[2 * h + 1] = turned[64:128]
    fr = RingReduce(net, place.z_dev, place.z_at, fz_out, fz_far, fz_near, f_cut)
    fr.start_far(gfilt[place.z_at(2)])
    fr.start_near(lambda rows: gfilt[(place.z_at(1),) + rows],
                  lambda rows: gfilt[(place.z_at(-1),) + rows])

    y_cut = ((pl.ds(0, 128),), (pl.ds(128, 128),))

    def weight_grad(slot, block):
        ring = RingReduce(net, place.y_dev, place.y_at, y_out.at[slot], y_far.at[slot],
                          y_near.at[slot], y_cut)
        ring.start_far(block(place.y_at(2)))
        keep_g[slot, 0] = block(place.y_at(1))
        keep_g[slot, 1] = block(place.y_at(-1))
        ring.start_near(lambda rows: keep_g[(slot, 0) + rows], lambda rows: keep_g[(slot, 1) + rows])
        keep_g[slot, 2] = block(place.y_at(0))
        return ring

    x_cut = ((pl.ds(0, 1),), (pl.ds(1, 1),))

    class Features:
        def __init__(self, slot, block):
            self.slot, self.swaps = slot, []
            for j, step in enumerate((2, 1, -1, 0)):
                feat[slot, j] = block(place.x_at(step)).reshape(4, 128, 256)
                c_out[slot, j] = feat[slot, j, pl.ds((1 - place.core) * 2, 2)].astype(bf16)
                self.swaps.append(net.copy(c_out.at[slot, j], c_in.at[slot, j], place.other_core()))

        def both(self, j, rows=(pl.ds(0, 2),)):
            lo, n = rows[0].start, rows[0].size
            return (feat[self.slot, j, pl.ds(place.core * 2 + lo, n)]
                    + c_in[self.slot, j, pl.ds(lo, n)].astype(f32))

        def ring(self):
            slot = self.slot
            self.reduce = RingReduce(net, place.x_dev, place.x_at, x_out.at[slot], x_far.at[slot],
                                     x_near.at[slot], x_cut)
            self.swaps[0].wait_recv()
            self.reduce.start_far(self.both(0))
            self.swaps[1].wait_recv()
            self.swaps[2].wait_recv()
            self.reduce.start_near(lambda rows: self.both(1, rows), lambda rows: self.both(2, rows))

        def relay(self):
            self.reduce.relay()

        def last(self):
            slot = self.slot
            self.swaps[3].wait_recv()
            fin_out[slot] = self.reduce.result(self.both(3)).astype(bf16)
            self.first = net.slots(2)
            for half in range(2):
                net.copy(fin_out.at[slot, half], fin_in.at[slot, place.zl], place.origin(half),
                         slot=self.first + place.zl, may_be_me=True)

        def result(self):
            for zl in range(2):
                net.arrived(fin_in.at[self.slot, zl], self.first + zl)
            return (fin_in[self.slot, 0].astype(f32) + fin_in[self.slot, 1].astype(f32)).astype(bf16)

    stores = []

    def put(value, stage, out):
        stage[...] = value
        copy = pltpu.make_async_copy(stage, out, local.at[len(stores)])
        copy.start()
        stores.append(copy)

    gathers[0].wait()
    mixed = Features(0, lambda b: dot(rows512(ag[0]), wo[b]))
    gathers[2].relay()
    turned_gated = jnp.transpose(rows512(ag[0]))
    grads = [weight_grad(0, lambda b: dot(turned_gated, rows512(cg[b])))]
    gathers[3].relay()
    turn(2)
    turn(3)
    fr.relay()
    gathers[1].wait()

    def in_grad(i):
        return weight_grad(i + 1, lambda b: dot(xt[b], rows512(ag[i + 1])))

    mixed.ring()
    grads.append(in_grad(0))
    grads[0].relay()
    gathers[2].wait()
    grads.append(in_grad(1))
    mixed.relay()
    fy[place.y] = fr.result(gfilt[place.zh]).astype(bf16)
    f_half = (pl.ds(0, 32), pl.ds(32, 32))
    fyg = RingGather(net, place.y_dev, place.y_at, lambda b: fy.at[b],
                     lambda b, h: fy.at[b, f_half[h]], fy.at[place.y])
    grads[1].relay()
    gathers[3].wait()
    left = side_by_side([rows512(ag[i + 1]) for i in range(3)])
    gtok = Features(1, lambda b: dot(left, side_by_side([wg[i, b] for i in range(3)]), 1, 1))
    gtok.ring()
    grads.append(in_grad(2))
    gtok.relay()
    mixed.last()
    grads[2].relay()
    fyg.relay()
    gtok.last()
    grads[3].relay()
    put(grads[0].result(keep_g[0, 2]), grads_v.at[3], gout_o)
    put(grads[1].result(keep_g[1, 2]), grads_v.at[0], gin_o.at[0])
    fyg.wait()
    fz[place.zh] = (fy[0].astype(f32) + fy[1].astype(f32) + fy[2].astype(f32)
                    + fy[3].astype(f32)).astype(bf16)
    fzg = RingGather(net, place.z_dev, place.z_at, lambda b: fz.at[b],
                     lambda b, h: fz.at[b, f_half[h]], fz.at[place.zh])
    put(mixed.result(), mixed_v, mixed_o)
    put(grads[2].result(keep_g[2, 2]), grads_v.at[1], gin_o.at[1])
    fzg.relay()
    put(grads[3].result(keep_g[3, 2]), grads_v.at[2], gin_o.at[2])
    put(gtok.result(), gtok_v, gtok_o)
    fzg.wait()
    put(fz[...].astype(f32), gfilt_v, gfilt_o)
    for copy in stores:
        copy.wait()
    net.finish()


def hand_on_kernel(*refs):
    sources, outs, stages, loads, stores = refs[:5], refs[5:10], refs[10:15], refs[15], refs[16]
    coming = [pltpu.make_async_copy(s, v, loads.at[i]) for i, (s, v) in enumerate(zip(sources, stages))]
    for copy in coming:
        copy.start()
    going = [pltpu.make_async_copy(v, o, stores.at[i]) for i, (v, o) in enumerate(zip(stages, outs))]
    for first, second in zip(coming, going):
        first.wait()
        second.start()
    for copy in going:
        copy.wait()


def vmem(*shape, kind=bf16):
    return pltpu.VMEM(shape, kind)


def shape_of(*shape, kind=bf16):
    return jax.ShapeDtypeStruct(shape, kind)


def in_vmem():
    return pl.BlockSpec(memory_space=pltpu.VMEM)


def in_place():
    return pl.BlockSpec(memory_space=pl.ANY)


results = (
    shape_of(128, 256), shape_of(128, 256), shape_of(3, 256, 256, kind=f32),
    shape_of(256, 256, kind=f32), shape_of(4, 64, 128, kind=f32))


def on_device(tokens, in_weight, out_weight, filters, cotangent):
    exchanged = pl.pallas_call(
        block_kernel,
        out_shape=results,
        in_specs=[in_vmem()] * 5,
        out_specs=(in_place(),) * 5,
        scratch_shapes=[
            vmem(4, 4, 128, 256), vmem(4, 4, 128, 256), vmem(3, 4, 256, 256), vmem(4, 256, 256),
            vmem(4, 256, 512),
            vmem(4, 4, 128, 256, kind=f32), vmem(4, 3, 128, 256), vmem(4, 2, 64, 256),
            vmem(4, 2, 128, 256), vmem(2, 128, 256), vmem(2, 128, 256), vmem(2, 128, 256),
            vmem(2, 16, 8, 128, kind=f32), vmem(2, 256, 128, kind=f32),
            vmem(8, 2, 256, 128, kind=f32), vmem(2, 16, 8, 128, kind=f32),
            vmem(4, 64, 128, kind=f32),
            vmem(4, 4, 128, 256), vmem(4, 3, 256, 256, kind=f32), vmem(4, 3, 256, 256),
            vmem(4, 2, 128, 256), vmem(4, 2, 256, 256),
            vmem(2, 4, 4, 128, 256, kind=f32), vmem(2, 4, 2, 128, 256), vmem(2, 4, 2, 128, 256),
            vmem(2, 3, 2, 128, 256), vmem(2, 2, 1, 128, 256), vmem(2, 2, 2, 128, 256),
            vmem(2, 2, 128, 256), vmem(2, 2, 128, 256),
            vmem(3, 64, 128), vmem(2, 32, 128), vmem(2, 64, 128), vmem(4, 64, 128),
            vmem(4, 64, 128),
            vmem(128, 256), vmem(128, 256), vmem(4, 256, 256, kind=f32),
            vmem(4, 64, 128, kind=f32),
            pltpu.SemaphoreType.DMA((176,)), pltpu.SemaphoreType.DMA((176,)),
            pltpu.SemaphoreType.DMA((8,))],
        compiler_params=pltpu.CompilerParams(
            collective_id=0, has_side_effects=True, vmem_limit_bytes=60 * 2 ** 20),
        name="block_exchange",
    )(tokens, cotangent, in_weight, out_weight, filters)
    mixed, grad_tokens, grad_in, grad_out, grad_filters = pl.pallas_call(
        hand_on_kernel,
        out_shape=results,
        in_specs=[in_place()] * 5,
        out_specs=(in_place(),) * 5,
        scratch_shapes=[pltpu.VMEM(r.shape, r.dtype) for r in results]
        + [pltpu.SemaphoreType.DMA((5,)), pltpu.SemaphoreType.DMA((5,))],
        name="hand_on",
    )(*exchanged)
    return mixed, grad_tokens, grad_in, grad_out, grad_filters.reshape(256, 128)


def solution(mesh):
    placed = (
        jax.P("seq", "fsdp"),
        jax.P(None, "seq", "fsdp"),
        jax.P("fsdp", "seq"),
        jax.P("fsdp", None),
        jax.P("seq", "fsdp"),
    )
    return jax.shard_map(
        on_device,
        mesh=mesh,
        in_specs=placed,
        out_specs=(
            jax.P("seq", "fsdp"),
            jax.P("seq", "fsdp"),
            jax.P(None, "seq", "fsdp"),
            jax.P("fsdp", "seq"),
            jax.P("fsdp", None),
        ),
        check_vma=False,
    )
```

time: 125 us -> 105 us (0.84)
  local copies, waits for them, and re-layouts: 10.4 us -> 0 us
  matrix products: 4.67 us -> 0 us
  Pallas kernels: 107 us -> 103 us
  other arithmetic: 1.39 us -> 0 us
    unnamed x16 -> x0, local copies, waits for them, and re-layouts: 6.44 us -> none
    conv_general_dilated x3 -> x0, matrix products: 4.67 us -> none  [the longest x1 1.86 us: filter_grad(): lax.conv_general_dilated(extended[None], gradient[:, None, :], (1,), 'VAL...]
    pallas_call x2, Pallas kernels: 107 us -> 103 us  [the longest x1 100 us: on_device(): pl.pallas_call(block_kernel, out_shape=results, in_specs=[in_vmem()] * 5,...]
    broadcast_in_dim x5 -> x0, local copies, waits for them, and re-layouts: 2.09 us -> none  [the longest x1 1.02 us: reverse_filter(): kernel = jnp.transpose(filters)[:, None, :]]
    another operation x3 -> x0, other arithmetic: 1.39 us -> none  [the longest x2 1.36 us: on_device(): jnp.stack([grad_gated * filtered, grad_signal * value_part, grad_signal *...]
where the time goes in v2:
time: 105 us; the launch traced here: 103 us
  Pallas kernels  103 us (98%)
    pallas_call x1, Pallas kernels, on_device(): pl.pallas_call(block_kernel, out_shape=results, in_specs=[in_vmem()] * 5,...  100 us
    pallas_call x1, Pallas kernels, on_device(): pl.pallas_call(hand_on_kernel, out_shape=results, in_specs=[in_place()] *...  2.3 us

profile of v2, /device:TPU:64, one launch (start us, length us, event | category | flops | bytes accessed | tf_op | source)
XLA Modules:
  0.0 103.4 jit_solution(2739085021328319141)
XLA Ops:
  0.6 100.5 %block_exchange.1 = (bf16[128,256]{1,0:T(8,128)(2,1)}, bf16[128,256]{1,0:T(8,128)(2,1)}, f32[3,256,256]{2,1,0:T(8,128)}, f32[256,256]{1,0:T(8,128)}, f32[4,64,128]{2,1,0:T(8,128)}) custom-call(bf16[128,256]{1,0:T(8,128)(2,1)} %tok.1, bf16[128,256]{1,0:T(8,128)(2,1)} %cot.1, bf16[3,256,256]{2,1,0:T(8,128)(2,1)} %win.1, bf16[256,256]{1,0:T(8,128)(2,1)} %wout.1, ...), custom_call_target="tpu_custom_call" | custom-call | tf_op jit(solution)/shard_map/block_exchange/pallas_call | solution.py:520
  101.1 2.3 %hand_on.1 = (bf16[128,256]{1,0:T(8,128)(2,1)}, bf16[128,256]{1,0:T(8,128)(2,1)}, f32[3,256,256]{2,1,0:T(8,128)}, f32[256,256]{1,0:T(8,128)}, f32[4,64,128]{2,1,0:T(8,128)}) custom-call(bf16[128,256]{1,0:T(8,128)(2,1)} %get-tuple-element.15.refs_0_, bf16[128,256]{1,0:T(8,128)(2,1)} %get-tuple-element.16.refs_1_, f32[3,256,256]{2,1,0:T(8,128)} %get-tuple-element.17.refs_2_, ...), custom_call_target="tpu_custom_call" | custom-call | tf_op jit(solution)/shard_map/hand_on/pallas_call | solution.py:548
